TPU v7x, 32 devices: a whole 2x2x4 slice. The times are simulated.
32 devices in a mesh: groups: 2 (over y), heads: 16 (over z, x, core).
Axes of the slice: x: 2, y: 2, z: 4, core: 2. Of those that a mesh axis runs over, the one named last changes fastest.
Arguments:
- query: bfloat16 [32, 16384], P('groups'), parts along dimension 0, may hold values from -4.5 to 4.5
- k_cache: bfloat16 [256, 1024, 128], P(('groups', 'heads')), parts along dimension 0, may hold values from -4.5 to 4.5
- v_cache: bfloat16 [256, 1024, 128], P(('groups', 'heads')), parts along dimension 0, may hold values from -40 to 40
- lengths: int32 [32], P('groups'), parts along dimension 0, may hold values from 1 to 1024, 5461 in all
- slots: int32 [32], P('groups'), parts along dimension 0, may hold values from 0 to 15, as said below
- gain: float32 [16384], replicated, may hold values from 0.1 to 1.9
- w_in: bfloat16 [8192, 16384], P('heads'), may hold values from -0.046875 to 0.046875
- w_out: bfloat16 [8192, 8192], P('heads'), may hold values from -0.09375 to 0.09375
Outputs:
- attn_out: bfloat16 [32, 16384], P(('groups', 'heads')), parts along dimension 0
- probe_out: bfloat16 [8192, 32], P('heads', 'groups'), parts along dimension 1
There are 2 independent parts, one for each index of `groups`. A program takes and returns all parts, laid end to end along the dimension named above; an argument that names none is the same for every part. Nothing has to cross between parts.
Inputs may be any that keep to these rules, and one draw needn't show every extreme that they name: slots is a permutation: each cache slot belongs to exactly one request. `lengths`: some request fills all 1024 positions.
All inputs are finite; a program needn't handle non-finite values.
Results may differ from a plain program's by a relative error of at most 0.007.
Values may be sent and summed in bfloat16 or wider, within the bound.
A program may use at most 64 MiB of HBM per device.

v0:
```python
import functools

import jax
import jax.numpy as jnp
from jax import lax
from jax.experimental import pallas as pl
from jax.experimental.pallas import tpu as pltpu
from jax.sharding import PartitionSpec as P

KVH = 8
DH = 128
GH = 16
WIDTH = GH * DH
F32 = jnp.float32
BF16 = jnp.bfloat16


def each(low, high, body):
    if high <= 16:
        for k in range(low, high):
            body(k)
    else:
        pl.loop(low, high)(body)


def xor(a, b, size):
    out, m = 0, 1
    while m < size:
        p, q = lax.rem(lax.div(a, jnp.int32(m)), jnp.int32(2)), b // m % 2
        out = out + m * (p + q - 2 * p * q)
        m *= 2
    return out


def kernel(
    count, block_out,
    slots_s, lengths_s, slots_row, q_hbm, gain_ref, k_hbm, v_hbm, win_hbm, wout_hbm,
    attn_ref, probe_ref,
    k_vm, v_vm, win_vm, wout_vm, stage, gath, acc, part, rs_send, rs_recv, q_vm, q_wide,
    k_sem, v_sem, win_sem, wout_sem, ag_send_sem, ag_recv_sem, rs_send_sem, rs_recv_sem, q_sem,
):
    me = lax.axis_index("heads")
    per_group = count // KVH
    group = me // per_group
    block = me % per_group
    slot_count, positions, _ = k_vm.shape
    requests = q_hbm.shape[0]
    po_loc = wout_hbm.shape[1] // count
    scale = 1.0 / DH**0.5

    q_cols = pl.ds(pl.multiple_of(group * WIDTH, WIDTH), WIDTH)
    q_copy = pltpu.make_async_copy(q_hbm.at[:, q_cols], q_vm, q_sem)
    q_copy.start()
    for c in range(slot_count):
        pltpu.make_async_copy(k_hbm.at[c], k_vm.at[c], k_sem.at[c]).start()
        pltpu.make_async_copy(v_hbm.at[c], v_vm.at[c], v_sem.at[c]).start()

    x_size = 4 if count % 128 == 0 else 2
    z_step = 2 * x_size
    x_hops = [2 * i for i in range(1, x_size)]
    z_hops = [z_step * i for i in range(1, count // z_step)]

    def group_of(j):
        return xor(group, j, KVH)

    def win_copy(j):
        cols = pl.ds(pl.multiple_of(group_of(j) * WIDTH, WIDTH), WIDTH)
        return pltpu.make_async_copy(win_hbm.at[:, cols], win_vm.at[j], win_sem.at[j])

    order = []
    for r in [0] + x_hops + z_hops + [a + b for a in z_hops for b in x_hops]:
        if r // per_group not in order:
            order.append(r // per_group)
    order += [j for j in range(KVH) if j not in order]
    wout_copy = pltpu.make_async_copy(wout_hbm, wout_vm, wout_sem)

    barrier = pltpu.get_barrier_semaphore()

    def greet(k):
        pl.semaphore_signal(
            barrier, inc=1, device_id={"heads": lax.rem(me + k, count)},
            device_id_type=pl.DeviceIdType.MESH,
        )

    each(1, count, greet)

    q_copy.wait()
    wanted = block * slot_count + lax.broadcasted_iota(jnp.int32, (slot_count, requests), 0)
    chosen = (jnp.broadcast_to(slots_row[...], (slot_count, requests)) == wanted).astype(BF16)
    q_wide[...] = jnp.dot(chosen, q_vm[...], preferred_element_type=F32)
    for c in range(slot_count):
        target = block * slot_count + c

        def find(r, found):
            return jnp.where(slots_s[r] == target, r, found)

        row = lax.fori_loop(0, requests, find, jnp.int32(0))
        q = jnp.concatenate(
            [q_wide[c : c + 1, h * DH : (h + 1) * DH] for h in range(GH)], axis=0
        ).astype(BF16)
        length = lengths_s[row]
        pltpu.make_async_copy(k_hbm.at[c], k_vm.at[c], k_sem.at[c]).wait()
        scores = lax.dot_general(
            q, k_vm[c], (((1,), (1,)), ((), ())), preferred_element_type=F32
        ) * scale
        live = lax.broadcasted_iota(jnp.int32, (GH, positions), 1) < length
        masked = jnp.where(live, scores, F32(-1e30))
        rmax = jnp.max(masked, axis=-1, keepdims=True)
        expw = jnp.where(live, jnp.exp(masked - rmax), F32(0.0))
        rsum = jnp.sum(expw, axis=-1, keepdims=True)
        pltpu.make_async_copy(v_hbm.at[c], v_vm.at[c], v_sem.at[c]).wait()
        if c == 0:
            for j in order[:2]:
                win_copy(j).start()
        elif c + 1 < KVH:
            win_copy(order[c + 1]).start()
        else:
            wout_copy.start()
        rout = jnp.dot(expw.astype(BF16), v_vm[c], preferred_element_type=F32)
        out = rout / rsum
        for h in range(GH):
            stage[c : c + 1, h * DH : (h + 1) * DH] = out[h : h + 1, :]
    gath[0] = stage[...].astype(BF16)

    pl.semaphore_wait(barrier, count - 1)
    started = []

    def forward(r, hop):
        copy = pltpu.make_async_remote_copy(
            src_ref=gath.at[r], dst_ref=gath.at[r + hop],
            send_sem=ag_send_sem.at[r + hop], recv_sem=ag_recv_sem.at[r + hop],
            device_id={"heads": xor(me, hop, count)},
            device_id_type=pl.DeviceIdType.MESH,
        )
        copy.start()
        started.append(copy)

    for hop in z_hops[1:] + z_hops[:1] + x_hops + [1]:
        forward(0, hop)
    here = {0}

    def arrive(r):
        if r in here:
            return
        here.add(r)
        pltpu.make_async_remote_copy(
            src_ref=gath.at[0], dst_ref=gath.at[r],
            send_sem=ag_send_sem.at[0], recv_sem=ag_recv_sem.at[r],
            device_id={"heads": xor(me, 1, count)},
            device_id_type=pl.DeviceIdType.MESH,
        ).wait_recv()
        if r % z_step == 0:
            for hop in x_hops:
                forward(r, hop)
        if r % 2 == 0:
            forward(r, 1)

    total = jnp.zeros((requests, 1), F32)
    for n, j in enumerate(order):
        if n == 1:
            for r in x_hops + z_hops:
                arrive(r)
        if n >= 2:
            for r in x_hops:
                arrive(r + z_hops[min(n - 2, len(z_hops) - 1)])
        for b in range(per_group):
            arrive(j * per_group + b)
        win_copy(j).wait()
        cols = pl.ds(pl.multiple_of(group_of(j) * WIDTH, WIDTH), WIDTH)
        act = gath[j * per_group : (j + 1) * per_group].astype(F32)
        act = act.reshape(requests, WIDTH)
        total = total + jnp.sum(act * act, axis=-1, keepdims=True)
        scaled = (act * gain_ref[:, cols]).astype(BF16)
        product = lax.dot_general(
            scaled, win_vm[j], (((1,), (1,)), ((), ())), preferred_element_type=F32
        )
        acc[...] = product if n == 0 else acc[...] + product

    mean_sq = total * F32(1.0 / (KVH * WIDTH))
    pre = acc[...] * lax.rsqrt(mean_sq + F32(1e-05))
    hidden = (0.5 * pre * (1.0 + lax.erf(pre * F32(0.5**0.5)))).astype(BF16)
    rows_i = lax.broadcasted_iota(jnp.int32, (requests, requests), 0)
    cols_i = lax.broadcasted_iota(jnp.int32, (requests, requests), 1)
    held = xor(lax.div(cols_i, slot_count), block, per_group) * slot_count
    held = held + lax.rem(cols_i, slot_count)
    slots_b = jnp.broadcast_to(slots_row[...], (requests, requests))
    slots_col = jnp.sum(
        jnp.where(rows_i == cols_i, slots_b, 0).astype(F32), axis=1, keepdims=True
    )
    perm = (slots_col == held.astype(F32)).astype(BF16)
    hidden = jnp.dot(perm, hidden, preferred_element_type=F32).astype(BF16)

    wout_copy.wait()

    def partial(d):
        at = (d * po_loc) // block_out
        cols = pl.ds(pl.multiple_of(at * block_out, block_out), block_out)
        return jnp.dot(hidden, wout_vm[:, cols], preferred_element_type=F32)

    def rs_copy(k):
        return pltpu.make_async_remote_copy(
            src_ref=rs_send.at[k], dst_ref=rs_recv.at[k],
            send_sem=rs_send_sem.at[k], recv_sem=rs_recv_sem.at[k],
            device_id={"heads": lax.rem(me + k, count)},
            device_id_type=pl.DeviceIdType.MESH,
        )

    def send_partial(k):
        rs_send[k] = partial(lax.rem(me + k, count)).astype(BF16)
        rs_copy(k).start()

    each(1, count, send_partial)

    part[...] = partial(me)

    own_rows = attn_ref.shape[0]
    first = me * own_rows
    sub_i = lax.broadcasted_iota(jnp.int32, (8, requests), 0)
    lane_i = lax.broadcasted_iota(jnp.int32, (8, requests), 1)
    slots_8 = jnp.broadcast_to(slots_row[...], (8, requests))
    mine = jnp.sum(
        jnp.where(lane_i == first + sub_i, slots_8, 0).astype(F32), axis=1, keepdims=True
    )
    pick = (mine == held[:8].astype(F32)).astype(BF16)
    for j in range(KVH):
        cols = pl.ds(pl.multiple_of(group_of(j) * WIDTH, WIDTH), WIDTH)
        act = gath[j * per_group : (j + 1) * per_group].astype(F32)
        act = act.reshape(requests, WIDTH).astype(BF16)
        rows = jnp.dot(pick, act, preferred_element_type=F32)
        attn_ref[:, cols] = rows[:own_rows].astype(BF16)

    def add_partial(k):
        rs_copy(k).wait_recv()
        part[...] += rs_recv[k].astype(F32)

    each(1, count, add_partial)

    probe_ref[...] = part[...]

    def sent(k):
        rs_copy(k).wait_send()

    each(1, count, sent)
    for copy in started:
        copy.wait_send()


def local(query, k_cache, v_cache, lengths, slots, gain, w_in, w_out):
    count = lax.axis_size("heads")
    index = lax.axis_index("heads")
    per_group = count // KVH
    group = index // per_group
    slot_count, positions, _ = k_cache.shape
    requests = query.shape[0]
    units = w_in.shape[0]
    outs = w_out.shape[1]
    po_loc = outs // count
    block_out = max(po_loc, 128)
    own_rows = requests // count
    vmem = pl.BlockSpec(memory_space=pltpu.VMEM)
    smem = pl.BlockSpec(memory_space=pltpu.SMEM)
    hbm = pl.BlockSpec(memory_space=pl.ANY)
    dma = pltpu.SemaphoreType.DMA
    attn_out, probe = pl.pallas_call(
        functools.partial(kernel, count, block_out),
        out_shape=(
            jax.ShapeDtypeStruct((own_rows, KVH * WIDTH), BF16),
            jax.ShapeDtypeStruct((requests, block_out), F32),
        ),
        in_specs=[smem, smem, vmem, hbm, vmem, hbm, hbm, hbm, hbm],
        out_specs=(vmem, vmem),
        scratch_shapes=[
            pltpu.VMEM((slot_count, positions, DH), BF16),
            pltpu.VMEM((slot_count, positions, DH), BF16),
            pltpu.VMEM((KVH, units, WIDTH), BF16),
            pltpu.VMEM((units, outs), BF16),
            pltpu.VMEM((slot_count, WIDTH), F32),
            pltpu.VMEM((count, slot_count, WIDTH), BF16),
            pltpu.VMEM((requests, units), F32),
            pltpu.VMEM((requests, block_out), F32),
            pltpu.VMEM((count, requests, block_out), BF16),
            pltpu.VMEM((count, requests, block_out), BF16),
            pltpu.VMEM((requests, WIDTH), BF16),
            pltpu.VMEM((slot_count, WIDTH), F32),
            dma((slot_count,)),
            dma((slot_count,)),
            dma((KVH,)),
            dma,
            dma((count,)),
            dma((count,)),
            dma((count,)),
            dma((count,)),
            dma,
        ],
        compiler_params=pltpu.CompilerParams(
            collective_id=0, has_side_effects=True, vmem_limit_bytes=58 * 1024 * 1024
        ),
    )(
        slots, lengths, slots.reshape(1, requests), query, gain.reshape(1, KVH * WIDTH),
        k_cache, v_cache, w_in, w_out,
    )
    probe_t = probe.T
    if block_out != po_loc:
        probe_t = lax.dynamic_slice_in_dim(probe_t, (index * po_loc) % block_out, po_loc, 0)
    return (attn_out, probe_t.astype(BF16))


def solution(mesh):
    placed = (
        P("groups", None),
        P(("groups", "heads"), None, None),
        P(("groups", "heads"), None, None),
        P("groups"),
        P("groups"),
        P(),
        P("heads", None),
        P("heads", None),
    )
    return jax.shard_map(
        local,
        mesh=mesh,
        in_specs=placed,
        out_specs=(P(("groups", "heads"), None), P("heads", "groups")),
        check_vma=False,
    )
```

profile of v0, /device:TPU:11, one launch (start us, length us, event | category | flops | bytes accessed | tf_op | source)
XLA Modules:
  0.0 32.7 jit_solution(14710400635991516582)
XLA Ops:
  0.6 29.1 %shard_map.95 = (bf16[1,16384]{1,0:T(2,128)(2,1)}, f32[16,512]{1,0:T(8,128)}) custom-call(s32[16]{0:T(128)} %slots_s.1, s32[16]{0:T(128)} %lengths_s.1, s32[1,16]{1,0:T(1,128)} %bitcast.5, bf16[16,16384]{1,0:T(8,128)(2,1)} %q_hbm.1, f32[1,16384]{1,0:T(1,128)} %bitcast.4, bf16[8,1024,128]{2,1,0:T(8,128)(2,1)} %k_hbm.1, bf16[8,1024,128]{2,1,0:T(8,128)(2,1)} %v_hbm.1, ...), custom_call_target="tpu_custom_call" | custom-call | tf_op jit(solution)/shard_map/pallas_call | solution.py:264
  29.8 1.4 %convert_bitcast_fusion = bf16[512,16]{0,1:T(8,128)(2,1)} fusion(f32[16,512]{1,0:T(8,128)} %get-tuple-element.5), kind=kLoop, calls=%fused_computation | loop fusion | flops 8192 | bytes 49152 | tf_op jit(solution)/shard_map/convert_element_type | solution.py:305
  31.1 1.5 %copy.11 = bf16[1,16384]{1,0:T(2,128)(2,1)} copy(bf16[1,16384]{1,0:T(2,128)(2,1)} %get-tuple-element.8) | data formatting | bytes 65536
where the time goes:
time: 33 us; the launch traced here: 32.7 us
  Pallas kernels  29.1 us (88%)
  local copies, waits for them, and re-layouts  1.54 us (5%)
  other arithmetic  1.37 us (4%)
  between operations  0.64 us (2%)
    pallas_call x1, Pallas kernels, local(): pl.pallas_call(functools.partial(kernel, count, block_out), out_shape=(ja...  29.1 us
    unnamed x1, local copies, waits for them, and re-layouts  1.54 us
    convert_element_type x1, other arithmetic, local(): return (attn_out, probe_t.astype(BF16))  1.37 us

commit v1 on v0

--- a/solution.py
+++ b/solution.py
@@ -34,10 +34,12 @@
 
 def kernel(
     count, block_out,
-    slots_s, lengths_s, slots_row, q_hbm, gain_ref, k_hbm, v_hbm, win_hbm, wout_hbm,
+    slots_hbm, lengths_hbm, q_hbm, gain_hbm, k_hbm, v_hbm, win_hbm, wout_hbm,
     attn_ref, probe_ref,
-    k_vm, v_vm, win_vm, wout_vm, stage, gath, acc, part, rs_send, rs_recv, q_vm, q_wide,
-    k_sem, v_sem, win_sem, wout_sem, ag_send_sem, ag_recv_sem, rs_send_sem, rs_recv_sem, q_sem,
+    k_vm, v_vm, win_vm, wout_vm, gath, acc, part, rs_send, rs_recv, q_vm,
+    slots_row, lengths_row, gain_ref,
+    k_sem, v_sem, win_sem, wout_sem, ag_send_sem, ag_recv_sem, rs_send_sem, rs_recv_sem,
+    q_sem, small_sem,
 ):
     me = lax.axis_index("heads")
     per_group = count // KVH
@@ -49,11 +51,17 @@
     scale = 1.0 / DH**0.5
 
     q_cols = pl.ds(pl.multiple_of(group * WIDTH, WIDTH), WIDTH)
+    slots_copy = pltpu.make_async_copy(slots_hbm, slots_row, small_sem.at[0])
+    lengths_copy = pltpu.make_async_copy(lengths_hbm, lengths_row, small_sem.at[1])
+    gain_copy = pltpu.make_async_copy(gain_hbm, gain_ref, small_sem.at[2])
     q_copy = pltpu.make_async_copy(q_hbm.at[:, q_cols], q_vm, q_sem)
+    k_copy = pltpu.make_async_copy(k_hbm, k_vm, k_sem)
+    v_copy = pltpu.make_async_copy(v_hbm, v_vm, v_sem)
+    slots_copy.start()
+    lengths_copy.start()
     q_copy.start()
-    for c in range(slot_count):
-        pltpu.make_async_copy(k_hbm.at[c], k_vm.at[c], k_sem.at[c]).start()
-        pltpu.make_async_copy(v_hbm.at[c], v_vm.at[c], v_sem.at[c]).start()
+    k_copy.start()
+    v_copy.start()
 
     x_size = 4 if count % 128 == 0 else 2
     z_step = 2 * x_size
@@ -84,43 +92,69 @@
 
     each(1, count, greet)
 
+    rows_q = slot_count * GH
+    slots_copy.wait()
+    lengths_copy.wait()
+    spread = (
+        lax.rem(lax.broadcasted_iota(jnp.int32, (requests, GH * requests), 1), requests)
+        == lax.broadcasted_iota(jnp.int32, (requests, GH * requests), 0)
+    ).astype(BF16)
+    slots_8 = jnp.broadcast_to(slots_row[...], (8, requests))
+    slots_wide = jnp.dot(
+        slots_8.astype(F32).astype(BF16), spread, preferred_element_type=F32
+    )[:1]
+    row_i = lax.broadcasted_iota(jnp.int32, (rows_q, GH * requests), 0)
+    col_i = lax.broadcasted_iota(jnp.int32, (rows_q, GH * requests), 1)
+    wanted = (block * slot_count + lax.div(row_i, GH)).astype(F32)
+    gather = (
+        (jnp.broadcast_to(slots_wide, (rows_q, GH * requests)) == wanted)
+        & (lax.rem(row_i, GH) == lax.div(col_i, requests))
+    ).astype(BF16)
+    row_r = lax.broadcasted_iota(jnp.int32, (rows_q, requests), 0)
+    owned = jnp.broadcast_to(slots_row[...], (rows_q, requests)) == (
+        block * slot_count + lax.div(row_r, GH)
+    )
+    lengths_col = jnp.sum(
+        jnp.where(owned, jnp.broadcast_to(lengths_row[...], (rows_q, requests)), 0).astype(F32),
+        axis=1, keepdims=True,
+    )
+    row_h = lax.broadcasted_iota(jnp.int32, (rows_q, rows_q), 0)
+    col_c = lax.broadcasted_iota(jnp.int32, (rows_q, rows_q), 1)
+    regroup = (
+        (lax.rem(row_h, slot_count) == lax.div(col_c, GH))
+        & (lax.div(row_h, slot_count) == lax.rem(col_c, GH))
+    ).astype(BF16)
+    place = lax.broadcasted_iota(jnp.int32, (GH, positions), 1).astype(F32)
+
     q_copy.wait()
-    wanted = block * slot_count + lax.broadcasted_iota(jnp.int32, (slot_count, requests), 0)
-    chosen = (jnp.broadcast_to(slots_row[...], (slot_count, requests)) == wanted).astype(BF16)
-    q_wide[...] = jnp.dot(chosen, q_vm[...], preferred_element_type=F32)
+    stacked = jnp.concatenate([q_vm[:, h * DH : (h + 1) * DH] for h in range(GH)], axis=0)
+    q_all = jnp.dot(gather, stacked, preferred_element_type=F32).astype(BF16)
+    k_copy.wait()
+    gain_copy.start()
+    for j in order:
+        win_copy(j).start()
+    weights, sums = [], []
     for c in range(slot_count):
-        target = block * slot_count + c
-
-        def find(r, found):
-            return jnp.where(slots_s[r] == target, r, found)
-
-        row = lax.fori_loop(0, requests, find, jnp.int32(0))
-        q = jnp.concatenate(
-            [q_wide[c : c + 1, h * DH : (h + 1) * DH] for h in range(GH)], axis=0
-        ).astype(BF16)
-        length = lengths_s[row]
-        pltpu.make_async_copy(k_hbm.at[c], k_vm.at[c], k_sem.at[c]).wait()
         scores = lax.dot_general(
-            q, k_vm[c], (((1,), (1,)), ((), ())), preferred_element_type=F32
+            q_all[c * GH : (c + 1) * GH], k_vm[c], (((1,), (1,)), ((), ())),
+            preferred_element_type=F32,
         ) * scale
-        live = lax.broadcasted_iota(jnp.int32, (GH, positions), 1) < length
+        live = place < lengths_col[c * GH : (c + 1) * GH]
         masked = jnp.where(live, scores, F32(-1e30))
         rmax = jnp.max(masked, axis=-1, keepdims=True)
         expw = jnp.where(live, jnp.exp(masked - rmax), F32(0.0))
-        rsum = jnp.sum(expw, axis=-1, keepdims=True)
-        pltpu.make_async_copy(v_hbm.at[c], v_vm.at[c], v_sem.at[c]).wait()
-        if c == 0:
-            for j in order[:2]:
-                win_copy(j).start()
-        elif c + 1 < KVH:
-            win_copy(order[c + 1]).start()
-        else:
-            wout_copy.start()
-        rout = jnp.dot(expw.astype(BF16), v_vm[c], preferred_element_type=F32)
-        out = rout / rsum
-        for h in range(GH):
-            stage[c : c + 1, h * DH : (h + 1) * DH] = out[h : h + 1, :]
-    gath[0] = stage[...].astype(BF16)
+        sums.append(jnp.sum(expw, axis=-1, keepdims=True))
+        weights.append(expw.astype(BF16))
+    v_copy.wait()
+    wout_copy.start()
+    outs = []
+    for c in range(slot_count):
+        rout = jnp.dot(weights[c], v_vm[c], preferred_element_type=F32)
+        outs.append((rout / sums[c]).astype(BF16))
+    by_head = jnp.dot(regroup, jnp.concatenate(outs, axis=0), preferred_element_type=F32)
+    gath[0] = jnp.concatenate(
+        [by_head[h * slot_count : (h + 1) * slot_count] for h in range(GH)], axis=1
+    ).astype(BF16)
 
     pl.semaphore_wait(barrier, count - 1)
     started = []
@@ -155,6 +189,7 @@
         if r % 2 == 0:
             forward(r, 1)
 
+    gain_copy.wait()
     total = jnp.zeros((requests, 1), F32)
     for n, j in enumerate(order):
         if n == 1:
@@ -217,7 +252,6 @@
     first = me * own_rows
     sub_i = lax.broadcasted_iota(jnp.int32, (8, requests), 0)
     lane_i = lax.broadcasted_iota(jnp.int32, (8, requests), 1)
-    slots_8 = jnp.broadcast_to(slots_row[...], (8, requests))
     mine = jnp.sum(
         jnp.where(lane_i == first + sub_i, slots_8, 0).astype(F32), axis=1, keepdims=True
     )
@@ -243,6 +277,11 @@
     each(1, count, sent)
     for copy in started:
         copy.wait_send()
+
+
+def finish(attn_in, probe_in, attn_out, probe_out):
+    attn_out[...] = attn_in[...]
+    probe_out[...] = probe_in[...].astype(BF16)
 
 
 def local(query, k_cache, v_cache, lengths, slots, gain, w_in, w_out):
@@ -258,32 +297,32 @@
     block_out = max(po_loc, 128)
     own_rows = requests // count
     vmem = pl.BlockSpec(memory_space=pltpu.VMEM)
-    smem = pl.BlockSpec(memory_space=pltpu.SMEM)
-    hbm = pl.BlockSpec(memory_space=pl.ANY)
+    hbm = pl.BlockSpec(memory_space=pltpu.HBM)
     dma = pltpu.SemaphoreType.DMA
-    attn_out, probe = pl.pallas_call(
+    attn_row, probe_sum = pl.pallas_call(
         functools.partial(kernel, count, block_out),
         out_shape=(
-            jax.ShapeDtypeStruct((own_rows, KVH * WIDTH), BF16),
-            jax.ShapeDtypeStruct((requests, block_out), F32),
+            pltpu.VMEM((own_rows, KVH * WIDTH), BF16),
+            pltpu.VMEM((requests, block_out), F32),
         ),
-        in_specs=[smem, smem, vmem, hbm, vmem, hbm, hbm, hbm, hbm],
+        in_specs=[hbm] * 8,
         out_specs=(vmem, vmem),
         scratch_shapes=[
             pltpu.VMEM((slot_count, positions, DH), BF16),
             pltpu.VMEM((slot_count, positions, DH), BF16),
             pltpu.VMEM((KVH, units, WIDTH), BF16),
             pltpu.VMEM((units, outs), BF16),
-            pltpu.VMEM((slot_count, WIDTH), F32),
             pltpu.VMEM((count, slot_count, WIDTH), BF16),
             pltpu.VMEM((requests, units), F32),
             pltpu.VMEM((requests, block_out), F32),
             pltpu.VMEM((count, requests, block_out), BF16),
             pltpu.VMEM((count, requests, block_out), BF16),
             pltpu.VMEM((requests, WIDTH), BF16),
-            pltpu.VMEM((slot_count, WIDTH), F32),
-            dma((slot_count,)),
-            dma((slot_count,)),
+            pltpu.VMEM((1, requests), jnp.int32),
+            pltpu.VMEM((1, requests), jnp.int32),
+            pltpu.VMEM((1, KVH * WIDTH), F32),
+            dma,
+            dma,
             dma((KVH,)),
             dma,
             dma((count,)),
@@ -291,18 +330,29 @@
             dma((count,)),
             dma((count,)),
             dma,
+            dma((3,)),
         ],
         compiler_params=pltpu.CompilerParams(
             collective_id=0, has_side_effects=True, vmem_limit_bytes=58 * 1024 * 1024
         ),
     )(
-        slots, lengths, slots.reshape(1, requests), query, gain.reshape(1, KVH * WIDTH),
-        k_cache, v_cache, w_in, w_out,
-    )
+        slots.reshape(1, requests), lengths.reshape(1, requests), query,
+        gain.reshape(1, KVH * WIDTH), k_cache, v_cache, w_in, w_out,
+    )
+    attn_out, probe = pl.pallas_call(
+        finish,
+        out_shape=(
+            jax.ShapeDtypeStruct((own_rows, KVH * WIDTH), BF16),
+            jax.ShapeDtypeStruct((requests, block_out), BF16),
+        ),
+        in_specs=[vmem, vmem],
+        out_specs=(vmem, vmem),
+        compiler_params=pltpu.CompilerParams(vmem_limit_bytes=4 * 1024 * 1024),
+    )(attn_row, probe_sum)
     probe_t = probe.T
     if block_out != po_loc:
         probe_t = lax.dynamic_slice_in_dim(probe_t, (index * po_loc) % block_out, po_loc, 0)
-    return (attn_out, probe_t.astype(BF16))
+    return (attn_out, probe_t)
 
 
 def solution(mesh):

time: 33 us -> 25.9 us (0.78)
  Pallas kernels: 29.1 us -> 25 us
  local copies, waits for them, and re-layouts: 1.54 us -> 0 us
  other arithmetic: 1.37 us -> 0 us
    pallas_call x1 -> x2, Pallas kernels: 29.1 us -> 25 us  [the longest x1 24.4 us: local(): pl.pallas_call(functools.partial(kernel, count, block_out), out_shape=(pl...]
    unnamed x1 -> x0, local copies, waits for them, and re-layouts: 1.54 us -> none
    convert_element_type x1 -> x0, other arithmetic: 1.37 us -> none  [local(): return (attn_out, probe_t.astype(BF16))]
where the time goes in v1:
time: 25.9 us; the launch traced here: 25.7 us
  Pallas kernels  25 us (97%)
  between operations  0.64 us (2%)
    pallas_call x1, Pallas kernels, local(): pl.pallas_call(functools.partial(kernel, count, block_out), out_shape=(pl...  24.4 us
    pallas_call x1, Pallas kernels, local(): pl.pallas_call(finish, out_shape=(jax.ShapeDtypeStruct((own_rows, KVH * W...  0.64 us

profile of v1, /device:TPU:11, one launch (start us, length us, event | category | flops | bytes accessed | tf_op | source)
XLA Modules:
  0.0 25.7 jit_solution(13610900892957303272)
XLA Ops:
  0.6 24.4 %shard_map.95 = (bf16[1,16384]{1,0:T(2,128)(2,1)S(1)}, f32[16,512]{1,0:T(8,128)S(1)}) custom-call(s32[1,16]{1,0:T(1,128)} %bitcast.5, s32[1,16]{1,0:T(1,128)} %bitcast.6, bf16[16,16384]{1,0:T(8,128)(2,1)} %q_hbm.1, f32[1,16384]{1,0:T(1,128)} %bitcast.4, bf16[8,1024,128]{2,1,0:T(8,128)(2,1)} %k_hbm.1, bf16[8,1024,128]{2,1,0:T(8,128)(2,1)} %v_hbm.1, ...), custom_call_target="tpu_custom_call" | custom-call | tf_op jit(solution)/shard_map/pallas_call | solution.py:302
  25.0 0.6 %shard_map.96 = (bf16[1,16384]{1,0:T(2,128)(2,1)}, bf16[16,512]{1,0:T(8,128)(2,1)}) custom-call(bf16[1,16384]{1,0:T(2,128)(2,1)S(1)} %get-tuple-element.6.attn_in, f32[16,512]{1,0:T(8,128)S(1)} %get-tuple-element.7.probe_in), custom_call_target="tpu_custom_call" | custom-call | tf_op jit(solution)/shard_map/pallas_call | solution.py:342

commit v2 on v1

--- a/solution.py
+++ b/solution.py
@@ -60,6 +60,7 @@
     slots_copy.start()
     lengths_copy.start()
     q_copy.start()
+    gain_copy.start()
     k_copy.start()
     v_copy.start()
 
@@ -130,7 +131,6 @@
     stacked = jnp.concatenate([q_vm[:, h * DH : (h + 1) * DH] for h in range(GH)], axis=0)
     q_all = jnp.dot(gather, stacked, preferred_element_type=F32).astype(BF16)
     k_copy.wait()
-    gain_copy.start()
     for j in order:
         win_copy(j).start()
     weights, sums = [], []

time: 25.9 us -> 24.8 us (0.958)
  the two profiles are of different devices: /device:TPU:11 before, /device:TPU:0 now
where the time goes in v2:
time: 24.8 us; the launch traced here: 24.7 us
  Pallas kernels  24 us (97%)
  between operations  0.64 us (3%)
    pallas_call x1, Pallas kernels, local(): pl.pallas_call(functools.partial(kernel, count, block_out), out_shape=(pl...  23.4 us
    pallas_call x1, Pallas kernels, local(): pl.pallas_call(finish, out_shape=(jax.ShapeDtypeStruct((own_rows, KVH * W...  0.64 us

profile of v2, /device:TPU:0, one launch (start us, length us, event | category | flops | bytes accessed | tf_op | source)
XLA Modules:
  0.0 24.7 jit_solution(13376163978117634481)
XLA Ops:
  0.6 23.4 %shard_map.95 = (bf16[1,16384]{1,0:T(2,128)(2,1)S(1)}, f32[16,512]{1,0:T(8,128)S(1)}) custom-call(s32[1,16]{1,0:T(1,128)} %bitcast.5, s32[1,16]{1,0:T(1,128)} %bitcast.6, bf16[16,16384]{1,0:T(8,128)(2,1)} %q_hbm.1, f32[1,16384]{1,0:T(1,128)} %bitcast.4, bf16[8,1024,128]{2,1,0:T(8,128)(2,1)} %k_hbm.1, bf16[8,1024,128]{2,1,0:T(8,128)(2,1)} %v_hbm.1, ...), custom_call_target="tpu_custom_call" | custom-call | tf_op jit(solution)/shard_map/pallas_call | solution.py:302
  24.0 0.6 %shard_map.96 = (bf16[1,16384]{1,0:T(2,128)(2,1)}, bf16[16,512]{1,0:T(8,128)(2,1)}) custom-call(bf16[1,16384]{1,0:T(2,128)(2,1)S(1)} %get-tuple-element.6.attn_in, f32[16,512]{1,0:T(8,128)S(1)} %get-tuple-element.7.probe_in), custom_call_target="tpu_custom_call" | custom-call | tf_op jit(solution)/shard_map/pallas_call | solution.py:342
